TPU v7x, 32 devices: a whole 2x2x4 slice. The times are simulated.
32 devices in a mesh: band: 4 (over y, x), region: 8 (over z, core).
Axes of the slice: x: 2, y: 2, z: 4, core: 2. Of those that a mesh axis runs over, the one named last changes fastest.
Arguments:
- fields: float32 [8192, 512], P(('band', 'region')), may hold values from -6 to 6
- send_list: int32 [4, 8, 4, 2], replicated, may hold values from -1 to 1, as said below
- departure: int32 [16, 8192], P(None, ('band', 'region')), may hold values from 0 to 1279, as said below
- hweight: float32 [16, 8192], P(None, ('band', 'region')), may hold values from -0.2 to 0.5
- base_level: int32 [128, 8192], P(None, ('band', 'region')), may hold values from 1 to 125
- vweight: float32 [4, 128, 8192], P(None, None, ('band', 'region')), may hold values from -0.25 to 0.75
- vertical_op: float32 [128, 128], replicated, may hold values from -0.4 to 2, as said below
Outputs:
- level_shards: float32 [512, 8192], P('region', 'band')
Inputs may be any that keep to these rules, and one draw needn't show every extreme that they name: send_list[b, r, d] names distinct block numbers of device (b, r), each block being 128 consecutive points of it; a list holds 1 to 2 numbers followed by -1 in the remaining entries, and in every draw some region's lists are all full. departure[c, p] indexes the extended rows of point p's device: below 256 the device's own point, else 256 + d * 2 * 128 + s for row s of part d; only rows delivered by an existing neighbour from a list entry that is not -1 are named. vertical_op[k, l] is zero where k and l differ by more than 2.
All inputs are finite; a program needn't handle non-finite values.
Results may differ from a plain program's by a relative error of at most 0.0003.
Values sent between devices are 32-bit elements; how exact they have to be, the bound alone decides.
No kernel may reach another device: no remote copies, remote signals or barrier semaphores. Data moves between devices by JAX's collectives and lax.ppermute only.
A program may use at most 64 MiB of HBM per device.

v0:
```python
import jax
import jax.numpy as jnp
from jax import lax
from jax.sharding import PartitionSpec as P

BLK = 128


exact_mode = lax.Precision.HIGHEST


def from_behind(block, axis, distance):
    devices = range(lax.axis_size(axis))
    route = [(i - distance, i) for i in devices if i - distance in devices]
    return lax.ppermute(block, axis, route)


def from_behind_2(block, axis, distance):
    devices = range(lax.axis_size(axis))
    route = [((i - distance) % len(devices), i) for i in devices]
    return lax.ppermute(block, axis, route)


def padded_2(x, sides, width):
    for axis, dim in sides:
        size, length = (lax.axis_size(axis), x.shape[dim])
        up = [(i, (i + 1) % size) for i in range(size - 1)]
        down = [(j, i) for i, j in up]
        last = lax.slice_in_dim(x, length - width, length, axis=dim)
        initial = lax.slice_in_dim(x, 0, width, axis=dim)
        before = lax.ppermute(last, axis, up)
        after = lax.ppermute(initial, axis, down)
        x = jnp.concatenate([before, x, after], axis=dim)
    return x


def pack_blocks(block_table, block_list):
    safe_list = jnp.maximum(block_list, 0)
    picked = jnp.take(block_table, safe_list, axis=0)
    keeping = (block_list >= 0)[:, None, None]
    picked = jnp.where(keeping, picked, jnp.zeros((), picked.dtype))
    return picked.reshape(-1, picked.shape[-1])


def column_update(extended, depart_block, hweight_block, base_block, vweight_block, vertical_op):
    stencil_len, point_count = depart_block.shape
    width_all = extended.shape[1]
    levels = vertical_op.shape[0]
    fields_count = width_all // levels
    picked = jnp.take(extended, depart_block.reshape(-1), axis=0).reshape(
        stencil_len, point_count, width_all
    )
    horizontal = jnp.sum(hweight_block[:, :, None] * picked, axis=0)
    stacked = jnp.transpose(horizontal).reshape(fields_count, levels, point_count)
    source_ids = jnp.arange(levels, dtype=jnp.int32)[None, :, None]
    level_weights = jnp.zeros((levels, levels, point_count), jnp.float32)
    for offset in range(4):
        target = (base_block + (offset - 1))[:, None, :]
        level_weights = level_weights + jnp.where(
            target == source_ids, vweight_block[offset][:, None, :], jnp.zeros((), jnp.float32)
        )
    interpolated = jnp.einsum("klp,flp->fkp", level_weights, stacked, precision=exact_mode)
    return interpolated.reshape(width_all, point_count)


def body(fields, send_list, departure, hweight, base_level, vweight, vertical_op):
    point_total, width_all = fields.shape
    levels = vertical_op.shape[0]
    block_table = fields.reshape(point_total // BLK, BLK, width_all)
    band_id = lax.axis_index("band")
    region_id = lax.axis_index("region")
    region_count = lax.axis_size("region")
    own_lists = send_list[band_id, region_id]
    from_north = from_behind(pack_blocks(block_table, own_lists[0]), "band", 1)
    from_south = from_behind(pack_blocks(block_table, own_lists[1]), "band", -1)
    from_west = from_behind_2(pack_blocks(block_table, own_lists[2]), "region", 1)
    from_east = from_behind_2(pack_blocks(block_table, own_lists[3]), "region", -1)
    extended = jnp.concatenate([fields, from_north, from_south, from_west, from_east], axis=0)
    step_points = min(128, point_total)

    def one_step(step_id, result):
        first_col = step_id * step_points
        updated = column_update(
            extended,
            lax.dynamic_slice_in_dim(departure, first_col, step_points, 1),
            lax.dynamic_slice_in_dim(hweight, first_col, step_points, 1),
            lax.dynamic_slice_in_dim(base_level, first_col, step_points, 1),
            lax.dynamic_slice_in_dim(vweight, first_col, step_points, 2),
            vertical_op,
        )
        return lax.dynamic_update_slice_in_dim(result, updated, first_col, 1)

    result = lax.fori_loop(
        0, point_total // step_points, one_step, jnp.zeros((width_all, point_total), jnp.float32)
    )
    shard_rows = lax.all_to_all(result, "region", split_axis=0, concat_axis=1, tiled=True)
    row_count = width_all // region_count
    padded = padded_2(shard_rows, (("region", 0),), 2)
    global_rows = region_id * row_count + jnp.arange(row_count, dtype=jnp.int32)
    level_ids = global_rows % levels
    operated = jnp.zeros(shard_rows.shape, jnp.float32)
    for offset in range(-2, 3):
        target = level_ids + offset
        valid = (target >= 0) & (target < levels)
        coeff = vertical_op[level_ids, jnp.clip(target, 0, levels - 1)]
        coeff = jnp.where(valid, coeff, jnp.zeros((), jnp.float32))
        operated = operated + coeff[:, None] * padded[2 + offset : 2 + offset + row_count, :]
    return operated


def solution(mesh):
    placed = (
        P(("band", "region"), None),
        P(),
        P(None, ("band", "region")),
        P(None, ("band", "region")),
        P(None, ("band", "region")),
        P(None, None, ("band", "region")),
        P(),
    )
    return jax.shard_map(
        body, mesh=mesh, in_specs=placed, out_specs=P("region", "band"), check_vma=False
    )
```

profile of v0, /device:TPU:1, one launch (start us, length us, event | category | flops | bytes accessed | tf_op | source)
XLA Modules:
  0.0 178.1 jit_solution(16740423676924799088)
XLA Ops:
  0.0 1.0 maximum_reduce_fusion
  1.0 1.0 compare_reduce_fusion
  2.0 1.6 gather_fusion.6
  3.6 0.9 select_select_fusion.3
  4.6 4.7 %collective-permute-start = (f32[256,512]{1,0:T(8,128)}, f32[256,512]{1,0:T(8,128)}, u32[]{:S(2)}, u32[]{:S(2)}) collective-permute-start(f32[256,512]{1,0:T(8,128)} %bitcast.11), channel_id=1, source_target_pairs={{0,8},{8,16},{16,24},{1,9},{9,17},{17,25},{2,10},{10,18},{18,26},{... | collective-permute-start | bytes 1572872 | tf_op jit(solution)/shard_map/ppermute | solution.py:15
  9.3 1.6 gather_fusion.7
  10.9 0.9 select_select_fusion.2
  11.9 1.3 collective-permute-start.1
  13.2 0.6 gather_fusion.8
  13.8 0.9 select_select_fusion.1
  14.8 2.1 %collective-permute-start.2 = (f32[256,512]{1,0:T(8,128)}, f32[256,512]{1,0:T(8,128)}, u32[]{:S(2)}, u32[]{:S(2)}) collective-permute-start(f32[256,512]{1,0:T(8,128)} %bitcast.13), channel_id=1, source_target_pairs={{7,0},{0,1},{1,2},{2,3},{3,4},{4,5},{5,6},{6,7},{15,8},{8,9},{9,10... | collective-permute-start | bytes 1572872 | tf_op jit(solution)/shard_map/ppermute | solution.py:21
  16.9 0.6 gather_fusion.9
  17.5 0.9 select_select_fusion
  18.4 0.0 collective-permute-start.3
  18.5 0.9 collective-permute-done
  19.4 1.1 constant_dynamic-update-slice_fusion.4
  20.5 12.1 %collective-permute-done.1 = f32[256,512]{1,0:T(8,128)} collective-permute-done((f32[256,512]{1,0:T(8,128)}, f32[256,512]{1,0:T(8,128)}, u32[]{:S(2)}, u32[]{:S(2)}) %collective-permute-start.1) | collective-permute-done | bytes 524320 | tf_op jit(solution)/shard_map/ppermute | solution.py:15
  32.6 1.1 constant_dynamic-update-slice_fusion.3
  33.7 1.1 constant_dynamic-update-slice_fusion.2
  34.8 1.1 constant_dynamic-update-slice_fusion.1
  35.9 0.8 broadcast_in_dim.186.clone
  36.7 112.9 %while.13 = (s32[]{:T(128)}, f32[512,256]{1,0:T(8,128)}, f32[16,256]{1,0:T(8,128)}, s32[16,256]{1,0:T(8,128)}, f32[1280,512]{1,0:T(8,128)S(1)}, /*index=5*/s32[1...) while((s32[]{:T(128)}, f32[512,256]{1,0:T(8,128)}, ...), condition=%wide.region_2.4_spmd, body=%wide.region_0.3_spmd.sunk | while | flops 126881800 | bytes 17125624 | solution.py:93
  36.7 0.7 compare_and_fusion.6
  37.4 8.9 %gather_fusion = f32[2048,512]{1,0:T(8,128)} fusion(f32[1280,512]{1,0:T(8,128)S(1)} %get-tuple-element.290, s32[2048]{0:T(1024)S(1)} %broadcast_clamp_fusion.2), kind=kCustom, calls=%fused_computation.1.clone.1 | custom fusion | bytes 8396800 | tf_op jit(solution)/shard_map/while/body/eval_jaxpr/jit(_take)/gather | solution.py:50
  46.3 0.7 constant_dynamic-slice_fusion.15
  47.0 2.6 %multiply_reduce_fusion.2 = f32[128,512]{1,0:T(8,128)S(1)} fusion(f32[16,128,512]{2,1,0:T(8,128)} %bitcast.59, f32[16,128]{1,0:T(8,128)S(1)} %constant_dynamic-slice_fusion.15, pred[16,128]{1,0:T(8,128)(4,1)S(1)} %get-tuple-element.250), kind=kLoop, calls=%fused_computation.31.clone.1 | loop fusion | flops 3080192 | bytes 4466688 | tf_op jit(solution)/shard_map/while/body/eval_jaxpr/reduce_sum | solution.py:53
  49.6 0.1 reshape.413
  49.7 1.0 constant_dynamic-slice_fusion.16
  50.7 0.1 copy.34
  50.8 0.1 copy.36
  50.9 0.1 copy.37
  51.0 0.1 copy.38
  51.1 0.9 constant_dynamic-slice_fusion.17
  51.9 0.1 copy.35
  52.1 40.2 %fusion.62 = f32[4,128,128]{1,0,2:T(4,128)S(1)} fusion(f32[4,128,128]{1,0,2:T(4,128)S(1)} %reshape.413, f32[128,128]{0,1:T(8,128)S(1)} %bitcast.71, s32[128,128]{0,1:T(8,128)S(1)} %get-tuple-element.252, f32[128,128]{0,1:T(8,128)S(1)} %bitcast.72, s32[128,128]{0,1:T(8,128)S(1)} %get-tuple-element.254, f32[128,128]{0,1:T(8,128)S(1)} %bitcast.73, ...), kind=kOutput, calls=%fused_computation.32.clone.2 | convolution fusion | flops 123731968 | bytes 1048576 | tf_op jit(solution)/shard_map/while/body/eval_jaxpr/klp,flp->fkp/dot_general | solution.py:62
  92.2 0.1 copy.39
  92.4 0.7 constant_dynamic-update-slice_fusion.9
  93.1 0.7 compare_and_fusion.6
  93.9 8.9 %gather_fusion = f32[2048,512]{1,0:T(8,128)} fusion(f32[1280,512]{1,0:T(8,128)S(1)} %get-tuple-element.290, s32[2048]{0:T(1024)S(1)} %broadcast_clamp_fusion.2), kind=kCustom, calls=%fused_computation.1.clone.1 | custom fusion | bytes 8396800 | tf_op jit(solution)/shard_map/while/body/eval_jaxpr/jit(_take)/gather | solution.py:50
  102.8 0.7 constant_dynamic-slice_fusion.15
  103.5 2.6 %multiply_reduce_fusion.2 = f32[128,512]{1,0:T(8,128)S(1)} fusion(f32[16,128,512]{2,1,0:T(8,128)} %bitcast.59, f32[16,128]{1,0:T(8,128)S(1)} %constant_dynamic-slice_fusion.15, pred[16,128]{1,0:T(8,128)(4,1)S(1)} %get-tuple-element.250), kind=kLoop, calls=%fused_computation.31.clone.1 | loop fusion | flops 3080192 | bytes 4466688 | tf_op jit(solution)/shard_map/while/body/eval_jaxpr/reduce_sum | solution.py:53
  106.1 0.1 reshape.413
  106.2 1.0 constant_dynamic-slice_fusion.16
  107.1 0.1 copy.34
  107.2 0.1 copy.36
  107.3 0.1 copy.37
  107.4 0.1 copy.38
  107.5 0.9 constant_dynamic-slice_fusion.17
  108.4 0.1 copy.35
  108.5 40.2 %fusion.62 = f32[4,128,128]{1,0,2:T(4,128)S(1)} fusion(f32[4,128,128]{1,0,2:T(4,128)S(1)} %reshape.413, f32[128,128]{0,1:T(8,128)S(1)} %bitcast.71, s32[128,128]{0,1:T(8,128)S(1)} %get-tuple-element.252, f32[128,128]{0,1:T(8,128)S(1)} %bitcast.72, s32[128,128]{0,1:T(8,128)S(1)} %get-tuple-element.254, f32[128,128]{0,1:T(8,128)S(1)} %bitcast.73, ...), kind=kOutput, calls=%fused_computation.32.clone.2 | convolution fusion | flops 123731968 | bytes 1048576 | tf_op jit(solution)/shard_map/while/body/eval_jaxpr/klp,flp->fkp/dot_general | solution.py:62
  148.7 0.1 copy.39
  148.9 0.7 constant_dynamic-update-slice_fusion.9
  149.6 6.4 %all-to-all-start = ((f32[8,64,256]{2,1,0:T(8,128)}), f32[8,64,256]{2,1,0:T(8,128)S(1)}, u32[]{:S(2)}, u32[]{:S(2)}) async-start(f32[8,64,256]{2,1,0:T(8,128)} %bitcast.70), calls=%async_computation | async-start | bytes 1048576 | tf_op jit(solution)/shard_map/all_to_all | solution.py:96
  156.0 0.8 gather_fusion.4
  156.8 0.8 gather_fusion.5
  157.6 0.8 gather_fusion.2
  158.4 0.8 gather_fusion.3
  159.2 0.8 gather_fusion.1
  160.1 10.3 %all-to-all-done = f32[8,64,256]{2,1,0:T(8,128)S(1)} async-done(((f32[8,64,256]{2,1,0:T(8,128)}), f32[8,64,256]{2,1,0:T(8,128)S(1)}, u32[]{:S(2)}, u32[]{:S(2)}) %all-to-all-start) | async-done | bytes 524320 | tf_op jit(solution)/shard_map/all_to_all | solution.py:96
  170.4 2.9 %collective-permute-start.5 = (f32[2,2048]{1,0:T(2,128)S(1)}, f32[2,2048]{1,0:T(2,128)S(1)}, u32[]{:S(2)}, u32[]{:S(2)}) collective-permute-start(f32[2,2048]{1,0:T(2,128)S(1)} %bitcast.78), channel_id=1, source_target_pairs={{1,0},{2,1},{3,2},{4,3},{5,4},{6,5},{7,6},{9,8},{10,9},{11,10},{12... | collective-permute-start | bytes 49160 | tf_op jit(solution)/shard_map/ppermute | solution.py:32
  173.3 2.7 %collective-permute-start.4 = (f32[2,2048]{1,0:T(2,128)S(1)}, f32[2,2048]{1,0:T(2,128)S(1)}, u32[]{:S(2)}, u32[]{:S(2)}) collective-permute-start(f32[2,2048]{1,0:T(2,128)S(1)} %bitcast.77), channel_id=1, source_target_pairs={{0,1},{1,2},{2,3},{3,4},{4,5},{5,6},{6,7},{8,9},{9,10},{10,11},{11... | collective-permute-start | bytes 49160 | tf_op jit(solution)/shard_map/ppermute | solution.py:31
  176.0 0.0 collective-permute-done.5
  176.1 0.8 collective-permute-done.4
  176.9 1.2 fusion.26
  (33 shorter events, 0.4 us)
Async XLA Ops:
  0.0 156.0 %copy-start = (f32[128,128]{1,0:T(8,128)S(1)}, f32[128,128]{1,0:T(8,128)}, u32[]{:S(2)}) copy-start(f32[128,128]{1,0:T(8,128)} %param.17) | copy-start | bytes 196612
  0.0 13.2 %copy-start.1 = (f32[256,512]{1,0:T(8,128)S(1)}, f32[256,512]{1,0:T(8,128)}, u32[]{:S(2)}) copy-start(f32[256,512]{1,0:T(8,128)} %param.11) | copy-start | bytes 1572868
  4.6 14.8 %collective-permute-start = (f32[256,512]{1,0:T(8,128)}, f32[256,512]{1,0:T(8,128)}, u32[]{:S(2)}, u32[]{:S(2)}) collective-permute-start(f32[256,512]{1,0:T(8,128)} %bitcast.11), channel_id=1, source_target_pairs={{0,8},{8,16},{16,24},{1,9},{9,17},{17,25},{2,10},{10,18},{18,26},{... | collective-permute-start | bytes 1572872 | tf_op jit(solution)/shard_map/ppermute | solution.py:15
  11.9 20.7 %collective-permute-start.1 = (f32[256,512]{1,0:T(8,128)}, f32[256,512]{1,0:T(8,128)}, u32[]{:S(2)}, u32[]{:S(2)}) collective-permute-start(f32[256,512]{1,0:T(8,128)} %bitcast.12), channel_id=1, source_target_pairs={{8,0},{16,8},{24,16},{9,1},{17,9},{25,17},{10,2},{18,10},{26,18},{... | collective-permute-start | bytes 1572872 | tf_op jit(solution)/shard_map/ppermute | solution.py:15
  14.8 18.9 %collective-permute-start.2 = (f32[256,512]{1,0:T(8,128)}, f32[256,512]{1,0:T(8,128)}, u32[]{:S(2)}, u32[]{:S(2)}) collective-permute-start(f32[256,512]{1,0:T(8,128)} %bitcast.13), channel_id=1, source_target_pairs={{7,0},{0,1},{1,2},{2,3},{3,4},{4,5},{5,6},{6,7},{15,8},{8,9},{9,10... | collective-permute-start | bytes 1572872 | tf_op jit(solution)/shard_map/ppermute | solution.py:21
  18.4 16.3 %collective-permute-start.3 = (f32[256,512]{1,0:T(8,128)}, f32[256,512]{1,0:T(8,128)}, u32[]{:S(2)}, u32[]{:S(2)}) collective-permute-start(f32[256,512]{1,0:T(8,128)} %bitcast.14), channel_id=1, source_target_pairs={{1,0},{2,1},{3,2},{4,3},{5,4},{6,5},{7,6},{0,7},{9,8},{10,9},{11,1... | collective-permute-start | bytes 1572872 | tf_op jit(solution)/shard_map/ppermute | solution.py:21
  149.6 20.8 %all-to-all-start = ((f32[8,64,256]{2,1,0:T(8,128)}), f32[8,64,256]{2,1,0:T(8,128)S(1)}, u32[]{:S(2)}, u32[]{:S(2)}) async-start(f32[8,64,256]{2,1,0:T(8,128)} %bitcast.70), calls=%async_computation | async-start | bytes 1048576 | tf_op jit(solution)/shard_map/all_to_all | solution.py:96
  170.4 5.6 %collective-permute-start.5 = (f32[2,2048]{1,0:T(2,128)S(1)}, f32[2,2048]{1,0:T(2,128)S(1)}, u32[]{:S(2)}, u32[]{:S(2)}) collective-permute-start(f32[2,2048]{1,0:T(2,128)S(1)} %bitcast.78), channel_id=1, source_target_pairs={{1,0},{2,1},{3,2},{4,3},{5,4},{6,5},{7,6},{9,8},{10,9},{11,10},{12... | collective-permute-start | bytes 49160 | tf_op jit(solution)/shard_map/ppermute | solution.py:32
  173.3 3.5 %collective-permute-start.4 = (f32[2,2048]{1,0:T(2,128)S(1)}, f32[2,2048]{1,0:T(2,128)S(1)}, u32[]{:S(2)}, u32[]{:S(2)}) collective-permute-start(f32[2,2048]{1,0:T(2,128)S(1)} %bitcast.77), channel_id=1, source_target_pairs={{0,1},{1,2},{2,3},{3,4},{4,5},{5,6},{6,7},{8,9},{9,10},{10,11},{11... | collective-permute-start | bytes 49160 | tf_op jit(solution)/shard_map/ppermute | solution.py:31
where the time goes:
time: 179 us; the launch traced here: 178 us
  matrix products  80.4 us (45%)
  local copies, waits for them, and re-layouts  39.3 us (22%)
  waiting for transfers between devices  24.1 us (13%)
  starting transfers between devices  20.1 us (11%)
  other arithmetic  13.8 us (8%)
    dot_general x2, matrix products, column_update(): jnp.einsum('klp,flp->fkp', level_weights, stacked, precision=exact_mode)  80.4 us
    gather x2, local copies, waits for them, and re-layouts, column_update(): jnp.take(extended, depart_block.reshape(-1), axis=0)  17.8 us
    ppermute x2, waiting for transfers between devices, from_behind(): return lax.ppermute(block, axis, route)  13 us
    all_to_all x1, waiting for transfers between devices, body(): lax.all_to_all(result, 'region', split_axis=0, concat_axis=1, tiled=True)  10.3 us
    all_to_all x1, starting transfers between devices, body(): lax.all_to_all(result, 'region', split_axis=0, concat_axis=1, tiled=True)  6.4 us
    ppermute x2, starting transfers between devices, from_behind(): return lax.ppermute(block, axis, route)  6 us
    reduce_sum x2, other arithmetic, column_update(): horizontal = jnp.sum(hweight_block[:, :, None] * picked, axis=0)  5.2 us
    gather x4, local copies, waits for them, and re-layouts, pack_blocks(): picked = jnp.take(block_table, safe_list, axis=0)  4.4 us
  transfers between devices with their start and end apart: 7, of which 4 were waited for; matrix products, arithmetic and copies ran while one was open for 7% of the time, Pallas kernels for 0%

commit v1 on v0

v1 whole, which is shorter than its diff:
```python
import jax
import jax.numpy as jnp
from jax import lax
from jax.experimental import pallas as pl
from jax.experimental.pallas import tpu as pltpu
from jax.sharding import PartitionSpec as P

BLK = 128
LANES = 128

VMEM = pltpu.MemorySpace.VMEM
SMEM = pltpu.MemorySpace.SMEM


def split(x):
    hi = x.astype(jnp.bfloat16)
    lo = (x - hi.astype(jnp.float32)).astype(jnp.bfloat16)
    return hi, lo


def mm(a, b, dims):
    return lax.dot_general(a, b, (dims, ((), ())), preferred_element_type=jnp.float32)


def mm3(a, b, dims):
    (ah, al), (bh, bl) = a, b
    return mm(ah, bh, dims) + (mm(ah, bl, dims) + mm(al, bh, dims))


def prep_kernel(
    own_blocks, list_len, ids, lists, dep, hw, base, vw, w_hi, w_lo, idx_out, vwt_out
):
    stencil, points = dep.shape
    list_blocks = 4 * list_len
    d = dep[...]
    block = d // BLK
    renamed = block
    for j in range(list_blocks):
        direction, slot = divmod(j, list_len)
        at = ids[direction] * list_blocks + direction * list_len + slot
        target = own_blocks * (1 + direction) + jnp.maximum(lists[at], 0)
        renamed = jnp.where(block == own_blocks + j, target, renamed)
    rows = renamed * BLK + (d - block * BLK)
    pad = LANES - stencil
    rows_t = jnp.concatenate([rows, jnp.zeros((pad, points), jnp.int32)], axis=0).T
    hw_t = jnp.concatenate([hw[...], jnp.zeros((pad, points), jnp.float32)], axis=0).T
    lane = lax.broadcasted_iota(jnp.int32, (points, LANES), 1)
    total = w_hi.shape[1]
    for j in range(total // LANES):
        acc = jnp.zeros((points, LANES), jnp.float32)
        for c in range(stencil):
            hit = (rows_t[:, c : c + 1] - j * LANES) == lane
            acc = acc + jnp.where(hit, hw_t[:, c : c + 1], 0.0)
        hi, lo = split(acc)
        w_hi[:, j * LANES : (j + 1) * LANES] = hi
        w_lo[:, j * LANES : (j + 1) * LANES] = lo
    idx_out[...] = base[...].T
    for m in range(4):
        vwt_out[m] = vw[m].T


def main_kernel(w_hi, w_lo, own, north, south, west, east, idx, vwt, op, out, hor, inter):
    points = own.shape[0]
    levels = op.shape[0]
    for i, part in enumerate((own, north, south, west, east)):
        cols = slice(i * points, (i + 1) * points)
        got = mm3((w_hi[:, cols], w_lo[:, cols]), split(part[...]), ((1,), (0,)))
        if i == 0:
            hor[...] = got
        else:
            hor[...] += got
    op_parts = split(op[...])
    for f in range(own.shape[1] // levels):
        cols = slice(f * levels, (f + 1) * levels)
        h = hor[:, cols]
        acc = jnp.zeros_like(h)
        for m in range(4):
            acc = acc + vwt[m] * jnp.take_along_axis(
                h, idx[...] + (m - 1), axis=1, mode="promise_in_bounds"
            )
        out[cols, :] = mm3(op_parts, split(acc), ((1,), (1,)))


def body(fields, send_list, departure, hweight, base_level, vweight, vertical_op):
    points, width = fields.shape
    levels = vertical_op.shape[0]
    band, region = lax.axis_index("band"), lax.axis_index("region")
    bands, regions = lax.axis_size("band"), lax.axis_size("region")
    list_len = send_list.shape[3]

    def shift(axis, size, step, wrap):
        if wrap:
            route = [((i - step) % size, i) for i in range(size)]
        else:
            route = [(i - step, i) for i in range(size) if 0 <= i - step < size]
        return lax.ppermute(fields, axis, route)

    north = shift("band", bands, 1, False)
    south = shift("band", bands, -1, False)
    west = shift("region", regions, 1, True)
    east = shift("region", regions, -1, True)
    senders = jnp.stack(
        [
            jnp.maximum(band - 1, 0) * regions + region,
            jnp.minimum(band + 1, bands - 1) * regions + region,
            band * regions + (region - 1) % regions,
            band * regions + (region + 1) % regions,
        ]
    ).astype(jnp.int32)
    f32, bf16 = jnp.float32, jnp.bfloat16
    total = 5 * points
    vm = pl.BlockSpec(memory_space=VMEM)
    sm = pl.BlockSpec(memory_space=SMEM)
    w_hi, w_lo, idx, vwt = pl.pallas_call(
        lambda *refs: prep_kernel(points // BLK, list_len, *refs),
        out_shape=(
            jax.ShapeDtypeStruct((points, total), bf16),
            jax.ShapeDtypeStruct((points, total), bf16),
            jax.ShapeDtypeStruct((points, levels), jnp.int32),
            jax.ShapeDtypeStruct((4, points, levels), f32),
        ),
        in_specs=[sm, sm, vm, vm, vm, vm],
        out_specs=(vm, vm, vm, vm),
        name="prep",
    )(senders, send_list.reshape(-1), departure, hweight, base_level, vweight)
    result = pl.pallas_call(
        main_kernel,
        out_shape=jax.ShapeDtypeStruct((width, points), f32),
        in_specs=[vm] * 10,
        out_specs=vm,
        scratch_shapes=[pltpu.VMEM((points, width), f32), pltpu.VMEM((points, levels), f32)],
        name="interp",
    )(w_hi, w_lo, fields, north, south, west, east, idx, vwt, vertical_op)
    return lax.all_to_all(result, "region", split_axis=0, concat_axis=1, tiled=True)


def solution(mesh):
    placed = (
        P(("band", "region"), None),
        P(),
        P(None, ("band", "region")),
        P(None, ("band", "region")),
        P(None, ("band", "region")),
        P(None, None, ("band", "region")),
        P(),
    )
    return jax.shard_map(
        body, mesh=mesh, in_specs=placed, out_specs=P("region", "band"), check_vma=False
    )
```

time: 179 us -> 55.7 us (0.31)
  the two profiles are of different devices: /device:TPU:1 before, /device:TPU:6 now
where the time goes in v1:
time: 55.7 us; the launch traced here: 55.4 us
  blocking collectives  20.3 us (36%)
  Pallas kernels  15.4 us (28%)
  waiting for transfers between devices  8.49 us (15%)
  starting transfers between devices  7.07 us (13%)
  local copies, waits for them, and re-layouts  3.41 us (6%)
  other arithmetic  0.65 us (1%)
    all_to_all x1, blocking collectives, body(): lax.all_to_all(result, 'region', split_axis=0, concat_axis=1, tiled=True)  20.3 us
    pallas_call x1, Pallas kernels, body(): pl.pallas_call(lambda *refs: prep_kernel(points // BLK, list_len, *refs),...  9.49 us
    ppermute x4, waiting for transfers between devices, shift(): return lax.ppermute(fields, axis, route)  8.49 us
    ppermute x4, starting transfers between devices, shift(): return lax.ppermute(fields, axis, route)  7.07 us
    pallas_call x1, Pallas kernels, body(): pl.pallas_call(main_kernel, out_shape=jax.ShapeDtypeStruct((width, points...  5.93 us
    unnamed x11, local copies, waits for them, and re-layouts  1.85 us
  transfers between devices with their start and end apart: 4, of which 1 were waited for; matrix products, arithmetic and copies ran while one was open for 3% of the time, Pallas kernels for 17%

profile of v1, /device:TPU:6, one launch (start us, length us, event | category | flops | bytes accessed | tf_op | source)
XLA Modules:
  0.0 55.4 jit_solution(5189375045634758446)
XLA Ops:
  0.0 0.0 collective-permute-start.2
  0.0 2.5 %collective-permute-start.1 = (f32[256,512]{1,0:T(8,128)}, f32[256,512]{1,0:T(8,128)S(1)}, u32[]{:S(2)}, u32[]{:S(2)}) collective-permute-start(f32[256,512]{1,0:T(8,128)} %own.1), channel_id=1, source_target_pairs={{8,0},{16,8},{24,16},{9,1},{17,9},{25,17},{10,2},{18,10},{26,18},{... | collective-permute-start | bytes 1572872 | tf_op jit(solution)/shard_map/ppermute | solution.py:96
  2.5 1.3 %collective-permute-start = (f32[256,512]{1,0:T(8,128)}, f32[256,512]{1,0:T(8,128)S(1)}, u32[]{:S(2)}, u32[]{:S(2)}) collective-permute-start(f32[256,512]{1,0:T(8,128)} %own.1), channel_id=1, source_target_pairs={{0,8},{8,16},{16,24},{1,9},{9,17},{17,25},{2,10},{10,18},{18,26},{... | collective-permute-start | bytes 1572872 | tf_op jit(solution)/shard_map/ppermute | solution.py:96
  3.8 3.3 %collective-permute-start.3 = (f32[256,512]{1,0:T(8,128)}, f32[256,512]{1,0:T(8,128)S(1)}, u32[]{:S(2)}, u32[]{:S(2)}) collective-permute-start(f32[256,512]{1,0:T(8,128)} %own.1), channel_id=1, source_target_pairs={{1,0},{2,1},{3,2},{4,3},{5,4},{6,5},{7,6},{0,7},{9,8},{10,9},{11,1... | collective-permute-start | bytes 1572872 | tf_op jit(solution)/shard_map/ppermute | solution.py:96
  7.1 0.0 copy-start.4
  7.1 0.7 %copy-done.4 = s32[4,8,4,2]{1,3,2,0:T(2,128)S(1)} copy-done((s32[4,8,4,2]{1,3,2,0:T(2,128)S(1)}, s32[4,8,4,2]{1,3,2,0:T(2,128)}, u32[]{:S(2)}) %copy-start.4) | copy-done | bytes 1048
  7.8 0.2 copy.9
  8.0 0.7 %reshape.6.refs_1_ = s32[256]{0:T(256)} reshape(s32[4,8,4,2]{3,2,1,0:T(4,128)S(1)} %copy.9) | data formatting | bytes 2048 | tf_op jit(solution)/shard_map/reshape | solution.py:125
  8.7 0.6 %pad_add_fusion.refs_0_ = s32[4]{0:T(128)} fusion(s32[1]{0:T(128)} %bitcast.3, s32[1]{0:T(128)} %bitcast.2, s32[1]{0:T(128)} %bitcast.1, s32[1]{0:T(128)} %bitcast), kind=kLoop, calls=%fused_computation | loop fusion | flops 12 | bytes 32 | tf_op jit(solution)/shard_map/stack | solution.py:102
  9.4 9.5 %prep.1 = (bf16[256,1280]{1,0:T(8,128)(2,1)}, bf16[256,1280]{1,0:T(8,128)(2,1)}, s32[256,128]{1,0:T(8,128)}, f32[4,256,128]{2,1,0:T(8,128)}) custom-call(s32[4]{0:T(128)} %pad_add_fusion.refs_0_, s32[256]{0:T(256)} %reshape.6.refs_1_, s32[16,256]{1,0:T(8,128)} %refs_2_.1, f32[16,256]{1,0:T(8,128)} %refs_3_.1, s32[128,256]{1,0:T(8,128)} %refs_4_.1, ...), custom_call_target="tpu_custom_call" | custom-call | tf_op jit(solution)/shard_map/prep/pallas_call | solution.py:114
  18.8 0.0 collective-permute-done.2.west
  18.8 0.0 copy-start
  18.9 0.0 collective-permute-done.1.south
  18.9 0.0 copy-start.1
  18.9 8.5 %collective-permute-done.north = f32[256,512]{1,0:T(8,128)S(1)} collective-permute-done((f32[256,512]{1,0:T(8,128)}, f32[256,512]{1,0:T(8,128)S(1)}, u32[]{:S(2)}, u32[]{:S(2)}) %collective-permute-start) | collective-permute-done | bytes 524320 | tf_op jit(solution)/shard_map/ppermute | solution.py:96
  27.4 0.0 copy-start.2
  27.4 0.0 collective-permute-done.3.east
  27.4 0.0 copy-start.3
  27.4 0.0 copy-done
  27.4 0.0 copy-done.1
  27.4 0.8 %copy-done.2 = f32[256,512]{1,0:T(8,128)} copy-done((f32[256,512]{1,0:T(8,128)}, f32[256,512]{1,0:T(8,128)S(1)}, u32[]{:S(2)}) %copy-start.2) | copy-done | bytes 524312
  28.2 0.2 copy-done.3
  28.3 5.9 %interp.1 = f32[512,256]{1,0:T(8,128)} custom-call(bf16[256,1280]{1,0:T(8,128)(2,1)} %get-tuple-element.9.w_hi, bf16[256,1280]{1,0:T(8,128)(2,1)} %get-tuple-element.10.w_lo, f32[256,512]{1,0:T(8,128)} %own.1, f32[256,512]{1,0:T(8,128)} %copy-done.2, f32[256,512]{1,0:T(8,128)} %copy-done.1, f32[256,512]{1,0:T(8,128)} %copy-done, f32[256,512]{1,0:T(8,128)} %copy-done.3, ...), custom_call_target="tpu_custom_call" | custom-call | tf_op jit(solution)/shard_map/interp/pallas_call | solution.py:126
  34.3 20.3 %all_to_all.19 = f32[8,64,256]{2,1,0:T(8,128)S(1)} all-to-all(f32[8,64,256]{2,1,0:T(8,128)} %bitcast.8), channel_id=1, replica_groups=mesh['band'=4,'region'=8] {'region'}, dimensions={0} | all-to-all | bytes 1048576 | tf_op jit(solution)/shard_map/all_to_all | solution.py:134
  54.6 0.8 %copy.11 = f32[8,8,8,256]{3,2,0,1:T(8,128)} copy(f32[8,8,8,256]{3,2,1,0:T(8,128)S(1)} %bitcast.9) | data formatting | bytes 1048576 | tf_op jit(solution)/shard_map/all_to_all | solution.py:134
Async XLA Ops:
  0.0 18.8 %collective-permute-start.2 = (f32[256,512]{1,0:T(8,128)}, f32[256,512]{1,0:T(8,128)S(1)}, u32[]{:S(2)}, u32[]{:S(2)}) collective-permute-start(f32[256,512]{1,0:T(8,128)} %own.1), channel_id=1, source_target_pairs={{7,0},{0,1},{1,2},{2,3},{3,4},{4,5},{5,6},{6,7},{15,8},{8,9},{9,10... | collective-permute-start | bytes 1572872 | tf_op jit(solution)/shard_map/ppermute | solution.py:96
  0.0 18.9 %collective-permute-start.1 = (f32[256,512]{1,0:T(8,128)}, f32[256,512]{1,0:T(8,128)S(1)}, u32[]{:S(2)}, u32[]{:S(2)}) collective-permute-start(f32[256,512]{1,0:T(8,128)} %own.1), channel_id=1, source_target_pairs={{8,0},{16,8},{24,16},{9,1},{17,9},{25,17},{10,2},{18,10},{26,18},{... | collective-permute-start | bytes 1572872 | tf_op jit(solution)/shard_map/ppermute | solution.py:96
  2.5 24.9 %collective-permute-start = (f32[256,512]{1,0:T(8,128)}, f32[256,512]{1,0:T(8,128)S(1)}, u32[]{:S(2)}, u32[]{:S(2)}) collective-permute-start(f32[256,512]{1,0:T(8,128)} %own.1), channel_id=1, source_target_pairs={{0,8},{8,16},{16,24},{1,9},{9,17},{17,25},{2,10},{10,18},{18,26},{... | collective-permute-start | bytes 1572872 | tf_op jit(solution)/shard_map/ppermute | solution.py:96
  3.8 23.6 %collective-permute-start.3 = (f32[256,512]{1,0:T(8,128)}, f32[256,512]{1,0:T(8,128)S(1)}, u32[]{:S(2)}, u32[]{:S(2)}) collective-permute-start(f32[256,512]{1,0:T(8,128)} %own.1), channel_id=1, source_target_pairs={{1,0},{2,1},{3,2},{4,3},{5,4},{6,5},{7,6},{0,7},{9,8},{10,9},{11,1... | collective-permute-start | bytes 1572872 | tf_op jit(solution)/shard_map/ppermute | solution.py:96
  7.1 0.7 %copy-start.4 = (s32[4,8,4,2]{1,3,2,0:T(2,128)S(1)}, s32[4,8,4,2]{1,3,2,0:T(2,128)}, u32[]{:S(2)}) copy-start(s32[4,8,4,2]{1,3,2,0:T(2,128)} %param.8) | copy-start | bytes 3076
  18.8 8.5 %copy-start = (f32[256,512]{1,0:T(8,128)}, f32[256,512]{1,0:T(8,128)S(1)}, u32[]{:S(2)}) copy-start(f32[256,512]{1,0:T(8,128)S(1)} %collective-permute-done.2.west) | copy-start | bytes 1572868
  18.9 8.5 %copy-start.1 = (f32[256,512]{1,0:T(8,128)}, f32[256,512]{1,0:T(8,128)S(1)}, u32[]{:S(2)}) copy-start(f32[256,512]{1,0:T(8,128)S(1)} %collective-permute-done.1.south) | copy-start | bytes 1572868
  27.4 0.8 %copy-start.2 = (f32[256,512]{1,0:T(8,128)}, f32[256,512]{1,0:T(8,128)S(1)}, u32[]{:S(2)}) copy-start(f32[256,512]{1,0:T(8,128)S(1)} %collective-permute-done.north) | copy-start | bytes 1572868
  27.4 1.0 %copy-start.3 = (f32[256,512]{1,0:T(8,128)}, f32[256,512]{1,0:T(8,128)S(1)}, u32[]{:S(2)}) copy-start(f32[256,512]{1,0:T(8,128)S(1)} %collective-permute-done.3.east) | copy-start | bytes 1572868

commit v2 on v1

--- a/solution.py
+++ b/solution.py
@@ -7,6 +7,7 @@
 
 BLK = 128
 LANES = 128
+STRIP = 16
 
 VMEM = pltpu.MemorySpace.VMEM
 SMEM = pltpu.MemorySpace.SMEM
@@ -44,22 +45,25 @@
     pad = LANES - stencil
     rows_t = jnp.concatenate([rows, jnp.zeros((pad, points), jnp.int32)], axis=0).T
     hw_t = jnp.concatenate([hw[...], jnp.zeros((pad, points), jnp.float32)], axis=0).T
-    lane = lax.broadcasted_iota(jnp.int32, (points, LANES), 1)
-    total = w_hi.shape[1]
-    for j in range(total // LANES):
-        acc = jnp.zeros((points, LANES), jnp.float32)
+    tiles = w_hi.shape[1] // LANES
+    lane = lax.broadcasted_iota(jnp.int32, (STRIP, LANES), 1)
+    for p in range(0, points, STRIP):
+        strip = slice(p, p + STRIP)
+        acc = [jnp.zeros((STRIP, LANES), jnp.float32) for _ in range(tiles)]
         for c in range(stencil):
-            hit = (rows_t[:, c : c + 1] - j * LANES) == lane
-            acc = acc + jnp.where(hit, hw_t[:, c : c + 1], 0.0)
-        hi, lo = split(acc)
-        w_hi[:, j * LANES : (j + 1) * LANES] = hi
-        w_lo[:, j * LANES : (j + 1) * LANES] = lo
+            row = jnp.broadcast_to(rows_t[strip, c : c + 1], (STRIP, LANES)) - lane
+            weight = jnp.broadcast_to(hw_t[strip, c : c + 1], (STRIP, LANES))
+            for j in range(tiles):
+                acc[j] = acc[j] + jnp.where(row == j * LANES, weight, 0.0)
+        for j in range(tiles):
+            cols = slice(j * LANES, (j + 1) * LANES)
+            w_hi[strip, cols], w_lo[strip, cols] = split(acc[j])
     idx_out[...] = base[...].T
     for m in range(4):
         vwt_out[m] = vw[m].T
 
 
-def main_kernel(w_hi, w_lo, own, north, south, west, east, idx, vwt, op, out, hor, inter):
+def main_kernel(w_hi, w_lo, own, north, south, west, east, idx, vwt, op, out, hor):
     points = own.shape[0]
     levels = op.shape[0]
     for i, part in enumerate((own, north, south, west, east)):
@@ -121,6 +125,7 @@
         ),
         in_specs=[sm, sm, vm, vm, vm, vm],
         out_specs=(vm, vm, vm, vm),
+        compiler_params=pltpu.CompilerParams(vmem_limit_bytes=8 << 20),
         name="prep",
     )(senders, send_list.reshape(-1), departure, hweight, base_level, vweight)
     result = pl.pallas_call(
@@ -128,7 +133,8 @@
         out_shape=jax.ShapeDtypeStruct((width, points), f32),
         in_specs=[vm] * 10,
         out_specs=vm,
-        scratch_shapes=[pltpu.VMEM((points, width), f32), pltpu.VMEM((points, levels), f32)],
+        scratch_shapes=[pltpu.VMEM((points, width), f32)],
+        compiler_params=pltpu.CompilerParams(vmem_limit_bytes=8 << 20),
         name="interp",
     )(w_hi, w_lo, fields, north, south, west, east, idx, vwt, vertical_op)
     return lax.all_to_all(result, "region", split_axis=0, concat_axis=1, tiled=True)

time: 55.7 us -> 51.7 us (0.928)
  Pallas kernels: 15.4 us -> 6.19 us
  waiting for transfers between devices: 8.49 us -> 12.7 us
  local copies, waits for them, and re-layouts: 3.41 us -> 5.26 us
  other arithmetic: 0.65 us -> 0.08 us
    pallas_call x1, Pallas kernels: 9.49 us -> 3.31 us  [body(): pl.pallas_call(lambda *refs: prep_kernel(points // BLK, list_len, *refs),...]
    ppermute x4, waiting for transfers between devices: 8.49 us -> 12.7 us  [shift(): return lax.ppermute(fields, axis, route)]
    pallas_call x1, Pallas kernels: 5.93 us -> 2.88 us  [body(): pl.pallas_call(main_kernel, out_shape=jax.ShapeDtypeStruct((width, points...]
    unnamed x11 -> x13, local copies, waits for them, and re-layouts: 1.85 us -> 4.27 us
    reshape x1, local copies, waits for them, and re-layouts: 0.73 us -> 0.15 us  [body(): send_list.reshape(-1)]
    another operation x1, other arithmetic: 0.65 us -> 0.08 us  [body(): jnp.stack([jnp.maximum(band - 1, 0) * regions + region, jnp.minimum(band...]
  transfers between devices with their start and end apart: 4 -> 4, of which waited for: 1 -> 1; matrix products, arithmetic and copies ran while one was open for 3% -> 2% of each run, Pallas kernels for 17% -> 6%
where the time goes in v2:
time: 51.7 us; the launch traced here: 51.2 us
  blocking collectives  19.8 us (38%)
  waiting for transfers between devices  12.7 us (25%)
  starting transfers between devices  7.07 us (14%)
  Pallas kernels  6.19 us (12%)
  local copies, waits for them, and re-layouts  5.26 us (10%)
    all_to_all x1, blocking collectives, body(): lax.all_to_all(result, 'region', split_axis=0, concat_axis=1, tiled=True)  19.8 us
    ppermute x4, waiting for transfers between devices, shift(): return lax.ppermute(fields, axis, route)  12.7 us
    ppermute x4, starting transfers between devices, shift(): return lax.ppermute(fields, axis, route)  7.07 us
    unnamed x13, local copies, waits for them, and re-layouts  4.27 us
    pallas_call x1, Pallas kernels, body(): pl.pallas_call(lambda *refs: prep_kernel(points // BLK, list_len, *refs),...  3.31 us
    pallas_call x1, Pallas kernels, body(): pl.pallas_call(main_kernel, out_shape=jax.ShapeDtypeStruct((width, points...  2.88 us
  transfers between devices with their start and end apart: 4, of which 1 were waited for; matrix products, arithmetic and copies ran while one was open for 2% of the time, Pallas kernels for 6%

profile of v2, /device:TPU:6, one launch (start us, length us, event | category | flops | bytes accessed | tf_op | source)
XLA Modules:
  0.0 51.2 jit_solution(8965491899216889331)
XLA Ops:
  0.0 0.0 copy-start
  0.0 0.0 collective-permute-start.2
  0.0 2.6 %collective-permute-start.1 = (f32[256,512]{1,0:T(8,128)}, f32[256,512]{1,0:T(8,128)S(1)}, u32[]{:S(2)}, u32[]{:S(2)}) collective-permute-start(f32[256,512]{1,0:T(8,128)} %own.1), channel_id=1, source_target_pairs={{8,0},{16,8},{24,16},{9,1},{17,9},{25,17},{10,2},{18,10},{26,18},{... | collective-permute-start | bytes 1572872 | tf_op jit(solution)/shard_map/ppermute | solution.py:100
  2.6 1.3 %collective-permute-start = (f32[256,512]{1,0:T(8,128)}, f32[256,512]{1,0:T(8,128)S(1)}, u32[]{:S(2)}, u32[]{:S(2)}) collective-permute-start(f32[256,512]{1,0:T(8,128)} %own.1), channel_id=1, source_target_pairs={{0,8},{8,16},{16,24},{1,9},{9,17},{17,25},{2,10},{10,18},{18,26},{... | collective-permute-start | bytes 1572872 | tf_op jit(solution)/shard_map/ppermute | solution.py:100
  3.9 3.2 %collective-permute-start.3 = (f32[256,512]{1,0:T(8,128)}, f32[256,512]{1,0:T(8,128)S(1)}, u32[]{:S(2)}, u32[]{:S(2)}) collective-permute-start(f32[256,512]{1,0:T(8,128)} %own.1), channel_id=1, source_target_pairs={{1,0},{2,1},{3,2},{4,3},{5,4},{6,5},{7,6},{0,7},{9,8},{10,9},{11,1... | collective-permute-start | bytes 1572872 | tf_op jit(solution)/shard_map/ppermute | solution.py:100
  7.1 0.9 %copy.9 = s32[4,8,4,2]{3,2,1,0:T(4,128)S(1)} copy(s32[4,8,4,2]{1,3,2,0:T(2,128)} %param.8) | data formatting | bytes 2048 | tf_op args[1]
  8.0 0.1 reshape.6.refs_1_
  8.1 0.1 pad_add_fusion.refs_0_
  8.2 0.0 copy-start.1
  8.2 1.0 %copy-done.1 = f32[4,128,256]{2,1,0:T(8,128)S(1)} copy-done((f32[4,128,256]{2,1,0:T(8,128)S(1)}, f32[4,128,256]{2,1,0:T(8,128)}, u32[]{:S(2)}) %copy-start.1) | copy-done | bytes 524312
  9.2 0.0 copy-start.2
  9.2 0.9 %copy-done.2 = s32[128,256]{1,0:T(8,128)S(1)} copy-done((s32[128,256]{1,0:T(8,128)S(1)}, s32[128,256]{1,0:T(8,128)}, u32[]{:S(2)}) %copy-start.2) | copy-done | bytes 131096
  10.2 0.0 copy-start.4
  10.2 0.7 %copy-done.4 = s32[16,256]{1,0:T(8,128)S(1)} copy-done((s32[16,256]{1,0:T(8,128)S(1)}, s32[16,256]{1,0:T(8,128)}, u32[]{:S(2)}) %copy-start.4) | copy-done | bytes 16408
  10.9 0.0 copy-start.5
  10.9 0.7 %copy-done.5 = f32[16,256]{1,0:T(8,128)S(1)} copy-done((f32[16,256]{1,0:T(8,128)S(1)}, f32[16,256]{1,0:T(8,128)}, u32[]{:S(2)}) %copy-start.5) | copy-done | bytes 16408
  11.6 0.0 copy-start.3
  11.6 3.3 %prep.1 = (bf16[256,1280]{1,0:T(8,128)(2,1)S(1)}, bf16[256,1280]{1,0:T(8,128)(2,1)S(1)}, s32[256,128]{1,0:T(8,128)S(1)}, f32[4,256,128]{2,1,0:T(8,128)S(1)}) custom-call(s32[4]{0:T(128)S(1)} %pad_add_fusion.refs_0_, s32[256]{0:T(256)S(1)} %reshape.6.refs_1_, s32[16,256]{1,0:T(8,128)S(1)} %copy-done.4, f32[16,256]{1,0:T(8,128)S(1)} %copy-done.5, ...), custom_call_target="tpu_custom_call" | custom-call | tf_op jit(solution)/shard_map/prep/pallas_call | solution.py:118
  14.9 0.0 collective-permute-done.2.west
  14.9 0.0 collective-permute-done.1.south
  14.9 12.7 %collective-permute-done.north = f32[256,512]{1,0:T(8,128)S(1)} collective-permute-done((f32[256,512]{1,0:T(8,128)}, f32[256,512]{1,0:T(8,128)S(1)}, u32[]{:S(2)}, u32[]{:S(2)}) %collective-permute-start) | collective-permute-done | bytes 524320 | tf_op jit(solution)/shard_map/ppermute | solution.py:100
  27.6 0.0 collective-permute-done.3.east
  27.6 0.0 copy-done
  27.6 0.0 copy-done.3
  27.6 2.9 %interp.1 = f32[512,256]{1,0:T(8,128)S(1)} custom-call(bf16[256,1280]{1,0:T(8,128)(2,1)S(1)} %get-tuple-element.9.w_hi, bf16[256,1280]{1,0:T(8,128)(2,1)S(1)} %get-tuple-element.10.w_lo, f32[256,512]{1,0:T(8,128)S(1)} %copy-done, f32[256,512]{1,0:T(8,128)S(1)} %collective-permute-done.north, f32[256,512]{1,0:T(8,128)S(1)} %collective-permute-done.1.south, ...), custom_call_target="tpu_custom_call" | custom-call | tf_op jit(solution)/shard_map/interp/pallas_call | solution.py:131
  30.5 19.8 %all_to_all.19 = f32[8,64,256]{2,1,0:T(8,128)S(1)} all-to-all(f32[8,64,256]{2,1,0:T(8,128)S(1)} %bitcast.8), channel_id=1, replica_groups=mesh['band'=4,'region'=8] {'region'}, dimensions={0} | all-to-all | bytes 1048576 | tf_op jit(solution)/shard_map/all_to_all | solution.py:140
  50.4 0.8 %copy.11 = f32[8,8,8,256]{3,2,0,1:T(8,128)} copy(f32[8,8,8,256]{3,2,1,0:T(8,128)S(1)} %bitcast.9) | data formatting | bytes 1048576 | tf_op jit(solution)/shard_map/all_to_all | solution.py:140
Async XLA Ops:
  0.0 27.6 %copy-start = (f32[256,512]{1,0:T(8,128)S(1)}, f32[256,512]{1,0:T(8,128)}, u32[]{:S(2)}) copy-start(f32[256,512]{1,0:T(8,128)} %own.1) | copy-start | bytes 1572868
  0.0 14.9 %collective-permute-start.2 = (f32[256,512]{1,0:T(8,128)}, f32[256,512]{1,0:T(8,128)S(1)}, u32[]{:S(2)}, u32[]{:S(2)}) collective-permute-start(f32[256,512]{1,0:T(8,128)} %own.1), channel_id=1, source_target_pairs={{7,0},{0,1},{1,2},{2,3},{3,4},{4,5},{5,6},{6,7},{15,8},{8,9},{9,10... | collective-permute-start | bytes 1572872 | tf_op jit(solution)/shard_map/ppermute | solution.py:100
  0.0 14.9 %collective-permute-start.1 = (f32[256,512]{1,0:T(8,128)}, f32[256,512]{1,0:T(8,128)S(1)}, u32[]{:S(2)}, u32[]{:S(2)}) collective-permute-start(f32[256,512]{1,0:T(8,128)} %own.1), channel_id=1, source_target_pairs={{8,0},{16,8},{24,16},{9,1},{17,9},{25,17},{10,2},{18,10},{26,18},{... | collective-permute-start | bytes 1572872 | tf_op jit(solution)/shard_map/ppermute | solution.py:100
  2.6 25.0 %collective-permute-start = (f32[256,512]{1,0:T(8,128)}, f32[256,512]{1,0:T(8,128)S(1)}, u32[]{:S(2)}, u32[]{:S(2)}) collective-permute-start(f32[256,512]{1,0:T(8,128)} %own.1), channel_id=1, source_target_pairs={{0,8},{8,16},{16,24},{1,9},{9,17},{17,25},{2,10},{10,18},{18,26},{... | collective-permute-start | bytes 1572872 | tf_op jit(solution)/shard_map/ppermute | solution.py:100
  3.9 23.7 %collective-permute-start.3 = (f32[256,512]{1,0:T(8,128)}, f32[256,512]{1,0:T(8,128)S(1)}, u32[]{:S(2)}, u32[]{:S(2)}) collective-permute-start(f32[256,512]{1,0:T(8,128)} %own.1), channel_id=1, source_target_pairs={{1,0},{2,1},{3,2},{4,3},{5,4},{6,5},{7,6},{0,7},{9,8},{10,9},{11,1... | collective-permute-start | bytes 1572872 | tf_op jit(solution)/shard_map/ppermute | solution.py:100
  8.2 1.0 %copy-start.1 = (f32[4,128,256]{2,1,0:T(8,128)S(1)}, f32[4,128,256]{2,1,0:T(8,128)}, u32[]{:S(2)}) copy-start(f32[4,128,256]{2,1,0:T(8,128)} %refs_5_.1) | copy-start | bytes 1572868
  9.2 0.9 %copy-start.2 = (s32[128,256]{1,0:T(8,128)S(1)}, s32[128,256]{1,0:T(8,128)}, u32[]{:S(2)}) copy-start(s32[128,256]{1,0:T(8,128)} %refs_4_.1) | copy-start | bytes 393220
  10.2 0.7 %copy-start.4 = (s32[16,256]{1,0:T(8,128)S(1)}, s32[16,256]{1,0:T(8,128)}, u32[]{:S(2)}) copy-start(s32[16,256]{1,0:T(8,128)} %refs_2_.1) | copy-start | bytes 49156
  10.9 0.7 %copy-start.5 = (f32[16,256]{1,0:T(8,128)S(1)}, f32[16,256]{1,0:T(8,128)}, u32[]{:S(2)}) copy-start(f32[16,256]{1,0:T(8,128)} %refs_3_.1) | copy-start | bytes 49156
  11.6 16.1 %copy-start.3 = (f32[128,128]{1,0:T(8,128)S(1)}, f32[128,128]{1,0:T(8,128)}, u32[]{:S(2)}) copy-start(f32[128,128]{1,0:T(8,128)} %op.1) | copy-start | bytes 196612
